TPU v7x, 256 devices: a whole 4x4x8 slice. The times are simulated.
256 devices in a mesh: dp: 64 (over z, y, core), group: 4 (over x).
Axes of the slice: x: 4, y: 4, z: 8, core: 2. Of those that a mesh axis runs over, the one named last changes fastest.
Arguments:
- frames: bfloat16 [4, 36864, 2048], P('group', 'dp'), may hold values from -6 to 6
- lengths: int32 [4, 192], P('group', 'dp'), may hold values from 24 to 192, as said below
- destination: int32 [4, 192], P('group', 'dp'), may hold values from 0 to 63, as said below
- offsets: int32 [4, 192], P('group', 'dp'), may hold values from 0 to 360, as said below
- norm_gain: bfloat16 [2048], P(('dp', 'group')), may hold values from 0.099609375 to 1.8984375
- weight_in: bfloat16 [2048, 4096], P(('dp', 'group')), may hold values from -0.125 to 0.125
- depth_kernel: bfloat16 [2048, 32], P(('dp', 'group')), may hold values from -1 to 1
- post_gain: bfloat16 [2048], P(('dp', 'group')), may hold values from 0.099609375 to 1.8984375
- weight_out: bfloat16 [2048, 2048], P(('dp', 'group')), may hold values from -0.125 to 0.125
Outputs:
- mixed: bfloat16 [4, 24576, 2048], P('group', 'dp')
Inputs may be any that keep to these rules, and one draw needn't show every extreme that they name: `destination`: every device of a group sends exactly one utterance to itself, one to dp index + 1 and one to dp index - 1, both taken modulo 64, within its own group index. `lengths`: every device receives utterances with 384 frames in all; one utterance of each device's receipts has exactly 192 frames; in every group some device's slots are full. `offsets`: the utterances that one device receives lie back to back without gaps or intersection over its 384 rows.
All inputs are finite; a program needn't handle non-finite values.
Results may differ from a plain program's by a relative error of at most 0.0085.
Values may be sent and summed in bfloat16 or wider, within the bound.
A program may use at most 128 MiB of HBM per device.

v0:
```python
import jax
import jax.numpy as jnp
from jax import lax
from jax.sharding import PartitionSpec as P

D = 2048
KERNEL = 32
MAXLEN = 192
RCV_DEV = 384
IN_CHUNKS = 4
OUT_CHUNKS = 2
epsilon = 1e-05


def shifted(array, axis, by):
    peers = lax.axis_size(axis)
    return lax.ppermute(array, axis, [(i, (i + by) % peers) for i in range(peers)])


def layer_norm(values, scale_gain):
    center = values - jnp.mean(values, axis=-1, keepdims=True)
    spread = jnp.mean(center * center, axis=-1, keepdims=True)
    return center * lax.rsqrt(spread + epsilon) * scale_gain.astype(jnp.float32)


def depth_pass(gated_rows, segment, kernel_rows):
    row_count = gated_rows.shape[0]
    margin = KERNEL // 2
    padded = jnp.pad(gated_rows, ((margin, margin), (0, 0)))
    labels = jnp.pad(segment, (margin, margin), constant_values=-1)
    depthwise = jnp.zeros_like(gated_rows)
    for column in range(KERNEL):
        inside = (labels[column : column + row_count] == segment)[:, None]
        depthwise = (
            depthwise
            + jnp.where(inside, padded[column : column + row_count], 0.0) * kernel_rows[:, column]
        )
    return depthwise


def relocate(own_part, next_part, prev_part):
    from_prev = shifted((next_part[0], next_part[1]), "dp", 1)
    from_next = shifted((prev_part[0], prev_part[1]), "dp", -1)
    received = jnp.zeros((RCV_DEV + MAXLEN, D), jnp.bfloat16)
    segment = jnp.zeros((RCV_DEV,), jnp.int32)
    position = jnp.arange(RCV_DEV, dtype=jnp.int32)
    arrivals = (own_part, from_prev, from_next)
    for label_id in range(3):
        frame_rows, meta_data = arrivals[label_id]
        current = lax.dynamic_slice_in_dim(received, meta_data[1], MAXLEN, 0)
        received = lax.dynamic_update_slice_in_dim(received, current + frame_rows, meta_data[1], 0)
        inside = (position >= meta_data[1]) & (position < meta_data[1] + meta_data[0])
        segment = jnp.where(inside, label_id + 1, segment)
    return (received[:RCV_DEV], segment)


def shards(
    frames, lengths, destination, offsets, norm_gain, weight_in, depth_kernel, post_gain, weight_out
):
    axes = ("dp", "group")
    small = jnp.concatenate(
        [norm_gain.reshape(-1, 1), post_gain.reshape(-1, 1), depth_kernel], axis=1
    )
    width = D // IN_CHUNKS
    in_parts = []
    for c in range(IN_CHUNKS):
        columns = [
            weight_in[:, c * width : (c + 1) * width],
            weight_in[:, D + c * width : D + (c + 1) * width],
        ]
        if c == 0:
            columns.append(small)
        in_parts.append(lax.all_gather(jnp.concatenate(columns, axis=1), axes, axis=0, tiled=True))
    small_all = in_parts[0][:, 2 * width :]
    in_parts[0] = in_parts[0][:, : 2 * width]
    out_width = D // OUT_CHUNKS
    out_parts = [
        lax.all_gather(weight_out[:, m * out_width : (m + 1) * out_width], axes, axis=0, tiled=True)
        for m in range(OUT_CHUNKS)
    ]
    norm_full = small_all[:, 0]
    post_full = small_all[:, 1]
    kernel_full = small_all[:, 2:].astype(jnp.float32)
    dp_count = lax.axis_size("dp")
    my_index = lax.axis_index("dp")
    local_frames = frames[0]
    lengths_here = lengths[0]
    dest_here = destination[0]
    offsets_here = offsets[0]
    starts = jnp.cumsum(lengths_here) - lengths_here
    relative = (dest_here - my_index) % dp_count
    slot_ids = jnp.arange(3, dtype=jnp.int32)

    def pick_entry(values, which):
        return jnp.sum(jnp.where(slot_ids == which, values, 0))

    def slot_of(code):
        return jnp.sum(jnp.where(relative == code, slot_ids, 0))

    chosen = (slot_of(0), slot_of(1), slot_of(dp_count - 1))

    def cut_utterance(source_rows, which):
        start_row = pick_entry(starts, which)
        live_count = pick_entry(lengths_here, which)
        frame_rows = lax.dynamic_slice_in_dim(source_rows, start_row, MAXLEN, 0)
        keep_rows = jnp.arange(MAXLEN, dtype=jnp.int32) < live_count
        kept = jnp.where(keep_rows[:, None], frame_rows, jnp.zeros_like(frame_rows))
        return (kept, jnp.stack([live_count, pick_entry(offsets_here, which)]))

    received, segment = relocate(
        cut_utterance(local_frames, chosen[0]),
        cut_utterance(local_frames, chosen[1]),
        cut_utterance(local_frames, chosen[2]),
    )
    source = received.astype(jnp.float32)
    normed = layer_norm(source, norm_full).astype(jnp.bfloat16)
    pieces = []
    for c in range(IN_CHUNKS):
        projected = jnp.dot(normed, in_parts[c], preferred_element_type=jnp.float32)
        gated = projected[:, :width] * jax.nn.sigmoid(projected[:, width:])
        pieces.append(depth_pass(gated, segment, kernel_full[c * width : (c + 1) * width]))
    depthwise = jnp.concatenate(pieces, axis=1)
    normed_post = layer_norm(depthwise, post_full)
    active = (normed_post * jax.nn.sigmoid(normed_post)).astype(jnp.bfloat16)
    outs = []
    for m in range(OUT_CHUNKS):
        mixed = source[:, m * out_width : (m + 1) * out_width] + jnp.dot(
            active, out_parts[m], preferred_element_type=jnp.float32
        )
        outs.append(mixed.astype(jnp.bfloat16))
    return jnp.concatenate(outs, axis=1)[None]


def solution(mesh):
    placed = (
        P("group", "dp", None),
        P("group", "dp"),
        P("group", "dp"),
        P("group", "dp"),
        P(("dp", "group")),
        P(("dp", "group"), None),
        P(("dp", "group"), None),
        P(("dp", "group")),
        P(("dp", "group"), None),
    )
    return jax.shard_map(
        shards, mesh=mesh, in_specs=placed, out_specs=P("group", "dp", None), check_vma=False
    )
```

profile of v0, /device:TPU:1, one launch (start us, length us, event | category | flops | bytes accessed | tf_op | source)
XLA Modules:
  0.0 724.6 jit_solution(8807620519260074038)
XLA Ops:
  16.1 3.3 select_reduce_fusion
  27.0 3.5 bitcast_select_fusion
  39.1 6.0 collective-permute-start.2
  48.5 4.0 dynamic_update_slice.9
  63.6 4.0 dynamic_update_slice.10
  69.1 4.6 dynamic_update_slice.11
  76.6 54.1 %all-gather.7.cloned.1.call-done = bf16[2048,1058]{1,0:T(8,128)(2,1)} async-done(((bf16[8,1058]{1,0:T(8,128)(2,1)}), bf16[2048,1058]{1,0:T(8,128)(2,1)}) %all-gather.7.cloned.1.call-update) | async-done | bytes 4333584 | tf_op jit(solution)/shard_map/all_gather | solution.py:73
  132.0 3.2 slice_reduce_fusion.122
  140.5 3.2 slice_reduce_fusion.124
  146.5 3.3 slice_reduce_fusion.123
  155.9 91.0 %all-gather.9.cloned.1.call-done = bf16[2048,1024]{1,0:T(8,128)(2,1)} async-done(((bf16[8,1024]{1,0:T(8,128)(2,1)}), bf16[2048,1024]{1,0:T(8,128)(2,1)}) %all-gather.9.cloned.1.call-update) | async-done | bytes 4194320 | tf_op jit(solution)/shard_map/all_gather | solution.py:73
  246.9 4.1 fusion.211
  252.0 111.0 %all-gather.11.cloned.1.call-done = bf16[2048,1024]{1,0:T(8,128)(2,1)} async-done(((bf16[8,1024]{1,0:T(8,128)(2,1)}), bf16[2048,1024]{1,0:T(8,128)(2,1)}) %all-gather.11.cloned.1.call-update) | async-done | bytes 4194320 | tf_op jit(solution)/shard_map/all_gather | solution.py:73
  363.0 4.1 fusion.210
  367.3 111.7 %all-gather.13.cloned.1.call-done = bf16[2048,1024]{1,0:T(8,128)(2,1)} async-done(((bf16[8,1024]{1,0:T(8,128)(2,1)}), bf16[2048,1024]{1,0:T(8,128)(2,1)}) %all-gather.13.cloned.1.call-update) | async-done | bytes 4194320 | tf_op jit(solution)/shard_map/all_gather | solution.py:73
  479.1 4.3 fusion.209
  484.1 6.0 fusion.213
  490.3 6.1 fusion.212
  496.4 5.3 fusion.214
  501.8 5.3 fusion.215
  510.3 84.7 %all-gather.17.cloned.1.call-done = bf16[2048,1024]{1,0:T(8,128)(2,1)} async-done(((bf16[8,1024]{1,0:T(8,128)(2,1)}), bf16[2048,1024]{1,0:T(8,128)(2,1)}) %all-gather.17.cloned.1.call-update) | async-done | bytes 4194320 | tf_op jit(solution)/shard_map/all_gather | solution.py:78
  595.0 5.6 fusion.220
  600.6 110.4 %all-gather.15.cloned.1.call-done = bf16[2048,1024]{1,0:T(8,128)(2,1)} async-done(((bf16[8,1024]{1,0:T(8,128)(2,1)}), bf16[2048,1024]{1,0:T(8,128)(2,1)}) %all-gather.15.cloned.1.call-update) | async-done | bytes 4194320 | tf_op jit(solution)/shard_map/all_gather | solution.py:78
  711.0 5.2 fusion.3
  (157 shorter events, 51.1 us)
Async XLA Ops:
  6.5 26.7 %copy-start.43 = (s32[1,3]{1,0:T(1,128)S(1)}, s32[1,3]{1,0:T(1,128)}, u32[]{:S(2)}) copy-start(s32[1,3]{1,0:T(1,128)} %param.12) | copy-start | bytes 40
  6.5 124.2 %all-gather.7.cloned.1.call-start = ((), (), s32[]{:S(2)}) async-start(), calls=%async_computation | async-start | bytes 4737024 | tf_op jit(solution)/shard_map/all_gather | solution.py:73
  10.2 236.6 %all-gather.9.cloned.1.call-start = ((), (), s32[]{:S(2)}) async-start(), calls=%async_computation.1 | async-start | bytes 4210688 | tf_op jit(solution)/shard_map/all_gather | solution.py:73
  11.0 352.0 %all-gather.11.cloned.1.call-start = ((), (), s32[]{:S(2)}) async-start(), calls=%async_computation.2 | async-start | bytes 4210688 | tf_op jit(solution)/shard_map/all_gather | solution.py:73
  11.7 467.3 %all-gather.13.cloned.1.call-start = ((), (), s32[]{:S(2)}) async-start(), calls=%async_computation.3 | async-start | bytes 4210688 | tf_op jit(solution)/shard_map/all_gather | solution.py:73
  12.4 582.6 %all-gather.17.cloned.1.call-start = ((), (), s32[]{:S(2)}) async-start(), calls=%async_computation.5 | async-start | bytes 4210688 | tf_op jit(solution)/shard_map/all_gather | solution.py:78
  13.8 697.2 %all-gather.15.cloned.1.call-start = ((), (), s32[]{:S(2)}) async-start(), calls=%async_computation.4 | async-start | bytes 4210688 | tf_op jit(solution)/shard_map/all_gather | solution.py:78
  30.6 31.6 %collective-permute-start.1 = (bf16[192,2048]{1,0:T(8,128)(2,1)}, bf16[192,2048]{1,0:T(8,128)(2,1)}, u32[]{:S(2)}, u32[]{:S(2)}) collective-permute-start(bf16[192,2048]{1,0:T(8,128)(2,1)} %get-tuple-element.159), channel_id=1, source_target_pairs={{0,4},{4,8},{8,12},{12,16},{16,20},{20,24},{24,28},{28,32},{32,36}... | collective-permute-start | bytes 2359304 | tf_op jit(solution)/shard_map/ppermute | solution.py:17
  38.4 16.1 %collective-permute-start = (s32[2]{0:T(128)S(1)}, s32[2]{0:T(128)S(1)}, u32[]{:S(2)}, u32[]{:S(2)}) collective-permute-start(s32[2]{0:T(128)S(1)} %get-tuple-element.205), channel_id=1, source_target_pairs={{0,4},{4,8},{8,12},{12,16},{16,20},{20,24},{24,28},{28,32},{32,36}... | collective-permute-start | bytes 32 | tf_op jit(solution)/shard_map/ppermute | solution.py:17
  38.4 29.2 %collective-permute-start.3 = (bf16[192,2048]{1,0:T(8,128)(2,1)}, bf16[192,2048]{1,0:T(8,128)(2,1)}, u32[]{:S(2)}, u32[]{:S(2)}) collective-permute-start(bf16[192,2048]{1,0:T(8,128)(2,1)} %get-tuple-element.157), channel_id=1, source_target_pairs={{0,252},{4,0},{8,4},{12,8},{16,12},{20,16},{24,20},{28,24},{32,28}... | collective-permute-start | bytes 2359304 | tf_op jit(solution)/shard_map/ppermute | solution.py:17
  39.1 13.4 %collective-permute-start.2 = (s32[2]{0:T(128)S(1)}, s32[2]{0:T(128)S(1)}, u32[]{:S(2)}, u32[]{:S(2)}) collective-permute-start(s32[2]{0:T(128)S(1)} %get-tuple-element.206), channel_id=1, source_target_pairs={{0,252},{4,0},{8,4},{12,8},{16,12},{20,16},{24,20},{28,24},{32,28}... | collective-permute-start | bytes 32 | tf_op jit(solution)/shard_map/ppermute | solution.py:17
  76.0 287.0 %copy-start.41 = (f32[384]{0:T(512)}, f32[384]{0:T(512)S(1)}, u32[]{:S(2)}) copy-start(f32[384]{0:T(512)S(1)} %broadcast_multiply_fusion) | copy-start | bytes 4612
  76.6 286.4 %copy-start.42 = (f32[384]{0:T(512)}, f32[384]{0:T(512)S(1)}, u32[]{:S(2)}) copy-start(f32[384]{0:T(512)S(1)} %add_rsqrt_fusion.1) | copy-start | bytes 4612
  140.5 9.3 %slice-start = ((s8[4718592]{0:T(1024)(128)(4,1)}), s8[4194304]{0:T(1024)(128)(4,1)S(1)}, s32[]{:S(2)}) async-start(s8[4718592]{0:T(1024)(128)(4,1)} %bitcast.63), calls=%async_computation.6 | async-start | bytes 8388608
  483.4 6.7 copy-start.1
  483.4 6.7 copy-start.3
  483.4 6.7 copy-start.4
  483.5 6.7 copy-start.5
  483.5 6.7 copy-start.6
  483.5 6.7 copy-start.7
  483.5 6.7 copy-start.22
  483.5 6.7 copy-start.23
  483.5 6.7 copy-start.24
  510.3 200.7 %copy-start = (f32[384,2048]{1,0:T(8,128)S(1)}, f32[384,2048]{1,0:T(8,128)}, u32[]{:S(2)}) copy-start(f32[384,2048]{1,0:T(8,128)} %slice_convert_fusion) | copy-start | bytes 9437188
  (32 other events, 182.8 us)
Sparse Core Ops, SparseCore 0:
  11.1 119.5 all-gather.6
  134.4 112.3 all-gather.8
  250.6 112.3 all-gather.10
  366.6 112.3 all-gather.12
  482.6 112.3 all-gather.16
  598.6 112.3 all-gather.14
where the time goes:
time: 730 us; the launch traced here: 725 us
  waiting for transfers between devices  563 us (77%)
  other arithmetic  57.6 us (8%)
  local copies, waits for them, and re-layouts  39.8 us (5%)
  between operations  29.5 us (4%)
  matrix products  25.1 us (3%)
  starting transfers between devices  9.56 us (1%)
    all_gather x4, waiting for transfers between devices, shards(): lax.all_gather(jnp.concatenate(columns, axis=1), axes, axis=0, tiled=True)  368 us
    all_gather x2, waiting for transfers between devices, shards(): lax.all_gather(weight_out[:, m * out_width:(m + 1) * out_width], axes, ax...  195 us
    reduce_sum x5, other arithmetic, layer_norm(): center = values - jnp.mean(values, axis=-1, keepdims=True)  23.1 us
    slice x7, local copies, waits for them, and re-layouts, depth_pass(): kernel_rows[:, column]  20.4 us
  transfers between devices with their start and end apart: 10, of which 6 were waited for; matrix products, arithmetic and copies ran while one was open for 15% of the time, Pallas kernels for 0%

commit v1 on v0

--- a/solution.py
+++ b/solution.py
@@ -70,7 +70,14 @@
         ]
         if c == 0:
             columns.append(small)
-        in_parts.append(lax.all_gather(jnp.concatenate(columns, axis=1), axes, axis=0, tiled=True))
+        in_parts.append(
+            jnp.concatenate(
+                lax.all_to_all(
+                    jnp.stack([jnp.concatenate(columns, axis=1)] * lax.axis_size(axes)), axes, 0, 0
+                ),
+                axis=0,
+            )
+        )
     small_all = in_parts[0][:, 2 * width :]
     in_parts[0] = in_parts[0][:, : 2 * width]
     out_width = D // OUT_CHUNKS

time: 730 us -> 589 us (0.81)
  the two profiles are of different devices: /device:TPU:1 before, /device:TPU:6 now
where the time goes in v1:
time: 589 us; the launch traced here: 579 us
  waiting for transfers between devices  372 us (63%)
  other arithmetic  53.5 us (9%)
  starting transfers between devices  50.7 us (9%)
  local copies, waits for them, and re-layouts  46.3 us (8%)
  between operations  29.8 us (5%)
  matrix products  27.3 us (5%)
    all_to_all x4, waiting for transfers between devices, shards(): lax.all_to_all(jnp.stack([jnp.concatenate(columns, axis=1)] * lax.axis_si...  290 us
    ppermute x4, waiting for transfers between devices, shifted(): lax.ppermute(array, axis, [(i, (i + by) % peers) for i in range(peers)])  81.9 us
    all_to_all x4, starting transfers between devices, shards(): lax.all_to_all(jnp.stack([jnp.concatenate(columns, axis=1)] * lax.axis_si...  43.4 us
    reduce_sum x5, other arithmetic, layer_norm(): center = values - jnp.mean(values, axis=-1, keepdims=True)  23.1 us
    slice x7, local copies, waits for them, and re-layouts, depth_pass(): kernel_rows[:, column]  20.3 us
    dot_general x4, matrix products, shards(): projected = jnp.dot(normed, in_parts[c], preferred_element_type=jnp.float32)  16.4 us
    dynamic_update_slice x3, local copies, waits for them, and re-layouts, relocate(): lax.dynamic_update_slice_in_dim(received, current + frame_rows, meta_data...  12.5 us
  transfers between devices with their start and end apart: 10, of which 5 were waited for; matrix products, arithmetic and copies ran while one was open for 19% of the time, Pallas kernels for 0%

profile of v1, /device:TPU:6, one launch (start us, length us, event | category | flops | bytes accessed | tf_op | source)
XLA Modules:
  0.0 579.2 jit_solution(16900344370729472405)
XLA Ops:
  9.8 15.6 %all-to-all-start.1 = ((bf16[256,8,1024]{2,1,0:T(8,128)(2,1)}), bf16[256,8,1024]{2,1,0:T(8,128)(2,1)}, u32[]{:S(2)}, u32[]{:S(2)}) async-start(bf16[256,8,1024]{2,1,0:T(8,128)(2,1)} %stack.27), calls=%async_computation.1 | async-start | bytes 8388608 | tf_op jit(solution)/shard_map/all_to_all | solution.py:75
  25.5 95.7 %all-to-all-done.1 = bf16[256,8,1024]{2,1,0:T(8,128)(2,1)} async-done(((bf16[256,8,1024]{2,1,0:T(8,128)(2,1)}), bf16[256,8,1024]{2,1,0:T(8,128)(2,1)}, u32[]{:S(2)}, u32[]{:S(2)}) %all-to-all-start.1) | async-done | bytes 4194336 | tf_op jit(solution)/shard_map/all_to_all | solution.py:75
  123.7 9.2 %all-to-all-start.2 = ((bf16[256,8,1024]{2,1,0:T(8,128)(2,1)}), bf16[256,8,1024]{2,1,0:T(8,128)(2,1)}, u32[]{:S(2)}, u32[]{:S(2)}) async-start(bf16[256,8,1024]{2,1,0:T(8,128)(2,1)} %stack.28), calls=%async_computation.2 | async-start | bytes 8388608 | tf_op jit(solution)/shard_map/all_to_all | solution.py:75
  133.2 95.4 %all-to-all-done.2 = bf16[256,8,1024]{2,1,0:T(8,128)(2,1)} async-done(((bf16[256,8,1024]{2,1,0:T(8,128)(2,1)}), bf16[256,8,1024]{2,1,0:T(8,128)(2,1)}, u32[]{:S(2)}, u32[]{:S(2)}) %all-to-all-start.2) | async-done | bytes 4194336 | tf_op jit(solution)/shard_map/all_to_all | solution.py:75
  231.2 9.1 %all-to-all-start = ((bf16[256,8,1058]{2,1,0:T(8,128)(2,1)}), bf16[256,8,1058]{2,1,0:T(8,128)(2,1)}, u32[]{:S(2)}, u32[]{:S(2)}) async-start(bf16[256,8,1058]{2,1,0:T(8,128)(2,1)} %stack.26), calls=%async_computation | async-start | bytes 9437184 | tf_op jit(solution)/shard_map/all_to_all | solution.py:75
  252.5 98.5 %all-to-all-done = bf16[256,8,1058]{2,1,0:T(8,128)(2,1)} async-done(((bf16[256,8,1058]{2,1,0:T(8,128)(2,1)}), bf16[256,8,1058]{2,1,0:T(8,128)(2,1)}, u32[]{:S(2)}, u32[]{:S(2)}) %all-to-all-start) | async-done | bytes 4333600 | tf_op jit(solution)/shard_map/all_to_all | solution.py:75
  353.6 9.4 %all-to-all-start.3 = ((bf16[256,8,1024]{2,1,0:T(8,128)(2,1)}), bf16[256,8,1024]{2,1,0:T(8,128)(2,1)}, u32[]{:S(2)}, u32[]{:S(2)}) async-start(bf16[256,8,1024]{2,1,0:T(8,128)(2,1)} %stack.29), calls=%async_computation.3 | async-start | bytes 8388608 | tf_op jit(solution)/shard_map/all_to_all | solution.py:75
  371.9 5.0 collective-permute-start.3
  380.8 4.0 dynamic_update_slice.9
  384.9 77.2 %collective-permute-done.2 = s32[2]{0:T(128)S(1)} collective-permute-done((s32[2]{0:T(128)S(1)}, s32[2]{0:T(128)S(1)}, u32[]{:S(2)}, u32[]{:S(2)}) %collective-permute-start.2) | collective-permute-done | bytes 40 | tf_op jit(solution)/shard_map/ppermute | solution.py:17
  464.0 4.7 collective-permute-done
  477.7 4.0 dynamic_update_slice.10
  483.2 4.4 dynamic_update_slice.11
  508.0 3.3 slice_reduce_fusion.123
  511.3 4.0 fusion
  519.0 4.0 fusion.6
  524.1 4.0 fusion.4
  528.6 4.4 fusion.2
  533.5 6.1 %fusion.216 = (f32[384]{0:T(512)S(1)}, f32[384,512]{1,0:T(8,128)S(1)}) fusion(f32[512]{0:T(512)S(1)} %copy-done.11, pred[384]{0:T(512)(128)(4,1)S(1)} %get-tuple-element.200, f32[512]{0:T(512)S(1)} %copy-done.12, pred[384]{0:T(512)(128)(4,1)S(1)} %get-tuple-element.171, f32[512]{0:T(512)S(1)} %copy-done.13, pred[384]{0:T(512)(128)(4,1)S(1)} %get-tuple-element.172, ...), kind=kLoop, calls=%fused_computation.499 | loop fusion | flops 18677376 | bytes 1651840 | tf_op jit(solution)/shard_map/reduce_sum | solution.py:21
  539.9 6.1 %fusion.215 = (f32[384]{0:T(512)S(1)}, f32[384,512]{1,0:T(8,128)S(1)}) fusion(f32[512]{0:T(512)S(1)} %copy-done.24, pred[384]{0:T(512)(128)(4,1)S(1)} %get-tuple-element.200, f32[512]{0:T(512)S(1)} %copy-done.25, pred[384]{0:T(512)(128)(4,1)S(1)} %get-tuple-element.171, f32[512]{0:T(512)S(1)} %copy-done.26, pred[384]{0:T(512)(128)(4,1)S(1)} %get-tuple-element.172, ...), kind=kLoop, calls=%fused_computation.498 | loop fusion | flops 18677376 | bytes 1651840 | tf_op jit(solution)/shard_map/reduce_sum | solution.py:21
  546.0 5.3 fusion.217
  551.3 5.3 fusion.218
  559.8 5.8 fusion.223
  565.6 5.1 fusion.9
  (166 shorter events, 63.5 us)
Async XLA Ops:
  9.8 111.4 %all-to-all-start.1 = ((bf16[256,8,1024]{2,1,0:T(8,128)(2,1)}), bf16[256,8,1024]{2,1,0:T(8,128)(2,1)}, u32[]{:S(2)}, u32[]{:S(2)}) async-start(bf16[256,8,1024]{2,1,0:T(8,128)(2,1)} %stack.27), calls=%async_computation.1 | async-start | bytes 8388608 | tf_op jit(solution)/shard_map/all_to_all | solution.py:75
  123.6 9.3 %copy-start.46 = (bf16[8]{0:T(256)(128)(2,1)S(1)}, bf16[8]{0:T(256)(128)(2,1)}, u32[]{:S(2)}) copy-start(bf16[8]{0:T(256)(128)(2,1)} %param.13) | copy-start | bytes 52
  123.7 9.4 %copy-start.47 = (bf16[8]{0:T(256)(128)(2,1)S(1)}, bf16[8]{0:T(256)(128)(2,1)}, u32[]{:S(2)}) copy-start(bf16[8]{0:T(256)(128)(2,1)} %param.16) | copy-start | bytes 52
  123.7 9.5 %copy-start.44 = (bf16[8,32]{1,0:T(8,128)(2,1)S(1)}, bf16[8,32]{1,0:T(8,128)(2,1)}, u32[]{:S(2)}) copy-start(bf16[8,32]{1,0:T(8,128)(2,1)} %param.15) | copy-start | bytes 1540
  123.7 105.0 %all-to-all-start.2 = ((bf16[256,8,1024]{2,1,0:T(8,128)(2,1)}), bf16[256,8,1024]{2,1,0:T(8,128)(2,1)}, u32[]{:S(2)}, u32[]{:S(2)}) async-start(bf16[256,8,1024]{2,1,0:T(8,128)(2,1)} %stack.28), calls=%async_computation.2 | async-start | bytes 8388608 | tf_op jit(solution)/shard_map/all_to_all | solution.py:75
  231.2 9.2 %copy-start.4 = (bf16[8,2048]{1,0:T(8,128)(2,1)S(1)}, bf16[8,2048]{1,0:T(8,128)(2,1)}, u32[]{:S(2)}) copy-start(bf16[8,2048]{1,0:T(8,128)(2,1)} %param.17) | copy-start | bytes 98308
  231.2 9.9 %copy-start.50 = (s32[1,3]{1,0:T(1,128)S(1)}, s32[1,3]{1,0:T(1,128)}, u32[]{:S(2)}) copy-start(s32[1,3]{1,0:T(1,128)} %param.10) | copy-start | bytes 40
  231.2 10.1 %copy-start.48 = (s32[1,3]{1,0:T(1,128)S(1)}, s32[1,3]{1,0:T(1,128)}, u32[]{:S(2)}) copy-start(s32[1,3]{1,0:T(1,128)} %param.11) | copy-start | bytes 40
  231.2 119.8 %all-to-all-start = ((bf16[256,8,1058]{2,1,0:T(8,128)(2,1)}), bf16[256,8,1058]{2,1,0:T(8,128)(2,1)}, u32[]{:S(2)}, u32[]{:S(2)}) async-start(bf16[256,8,1058]{2,1,0:T(8,128)(2,1)} %stack.26), calls=%async_computation | async-start | bytes 9437184 | tf_op jit(solution)/shard_map/all_to_all | solution.py:75
  240.3 319.5 %all-gather.5.cloned.1.call-start = ((), (), s32[]{:S(2)}) async-start(), calls=%async_computation.5 | async-start | bytes 4210688 | tf_op jit(solution)/shard_map/all_gather | solution.py:85
  353.6 9.5 %copy-start.3 = (bf16[1,576,2048]{2,1,0:T(8,128)(2,1)S(1)}, bf16[1,576,2048]{2,1,0:T(8,128)(2,1)}, u32[]{:S(2)}) copy-start(bf16[1,576,2048]{2,1,0:T(8,128)(2,1)} %param.9) | copy-start | bytes 7077892
  353.6 174.8 %all-to-all-start.3 = ((bf16[256,8,1024]{2,1,0:T(8,128)(2,1)}), bf16[256,8,1024]{2,1,0:T(8,128)(2,1)}, u32[]{:S(2)}, u32[]{:S(2)}) async-start(bf16[256,8,1024]{2,1,0:T(8,128)(2,1)} %stack.29), calls=%async_computation.3 | async-start | bytes 8388608 | tf_op jit(solution)/shard_map/all_to_all | solution.py:75
  363.0 202.5 %all-gather.3.cloned.1.call-start = ((), (), s32[]{:S(2)}) async-start(), calls=%async_computation.4 | async-start | bytes 4210688 | tf_op jit(solution)/shard_map/all_gather | solution.py:85
  365.0 111.2 %collective-permute-start.1 = (bf16[192,2048]{1,0:T(8,128)(2,1)}, bf16[192,2048]{1,0:T(8,128)(2,1)}, u32[]{:S(2)}, u32[]{:S(2)}) collective-permute-start(bf16[192,2048]{1,0:T(8,128)(2,1)} %get-tuple-element.159), channel_id=1, source_target_pairs={{0,4},{4,8},{8,12},{12,16},{16,20},{20,24},{24,28},{28,32},{32,36}... | collective-permute-start | bytes 2359304 | tf_op jit(solution)/shard_map/ppermute | solution.py:17
  370.4 98.2 %collective-permute-start = (s32[2]{0:T(128)S(1)}, s32[2]{0:T(128)S(1)}, u32[]{:S(2)}, u32[]{:S(2)}) collective-permute-start(s32[2]{0:T(128)S(1)} %get-tuple-element.205), channel_id=1, source_target_pairs={{0,4},{4,8},{8,12},{12,16},{16,20},{20,24},{24,28},{28,32},{32,36}... | collective-permute-start | bytes 32 | tf_op jit(solution)/shard_map/ppermute | solution.py:17
  371.9 109.9 %collective-permute-start.3 = (bf16[192,2048]{1,0:T(8,128)(2,1)}, bf16[192,2048]{1,0:T(8,128)(2,1)}, u32[]{:S(2)}, u32[]{:S(2)}) collective-permute-start(bf16[192,2048]{1,0:T(8,128)(2,1)} %get-tuple-element.157), channel_id=1, source_target_pairs={{0,252},{4,0},{8,4},{12,8},{16,12},{20,16},{24,20},{28,24},{32,28}... | collective-permute-start | bytes 2359304 | tf_op jit(solution)/shard_map/ppermute | solution.py:17
  376.9 85.2 %collective-permute-start.2 = (s32[2]{0:T(128)S(1)}, s32[2]{0:T(128)S(1)}, u32[]{:S(2)}, u32[]{:S(2)}) collective-permute-start(s32[2]{0:T(128)S(1)} %get-tuple-element.206), channel_id=1, source_target_pairs={{0,252},{4,0},{8,4},{12,8},{16,12},{20,16},{24,20},{28,24},{32,28}... | collective-permute-start | bytes 32 | tf_op jit(solution)/shard_map/ppermute | solution.py:17
  487.9 36.2 %copy-start.43 = (f32[384]{0:T(512)}, f32[384]{0:T(512)S(1)}, u32[]{:S(2)}) copy-start(f32[384]{0:T(512)S(1)} %broadcast_multiply_fusion) | copy-start | bytes 4612
  488.4 35.7 %copy-start.45 = (f32[384]{0:T(512)}, f32[384]{0:T(512)S(1)}, u32[]{:S(2)}) copy-start(f32[384]{0:T(512)S(1)} %add_rsqrt_fusion.1) | copy-start | bytes 4612
  532.9 6.7 %copy-start.1 = (f32[384,512]{1,0:T(8,128)S(1)}, f32[384,512]{1,0:T(8,128)}, u32[]{:S(2)}) copy-start(f32[384,512]{1,0:T(8,128)} %fusion.21) | copy-start | bytes 2359300
  532.9 6.7 %copy-start.5 = (f32[512]{0:T(512)S(1)}, f32[512]{0:T(512)}, u32[]{:S(2)}) copy-start(f32[512]{0:T(512)} %get-tuple-element.104) | copy-start | bytes 6148
  532.9 6.7 %copy-start.6 = (f32[512]{0:T(512)S(1)}, f32[512]{0:T(512)}, u32[]{:S(2)}) copy-start(f32[512]{0:T(512)} %get-tuple-element.105) | copy-start | bytes 6148
  533.0 6.7 %copy-start.7 = (f32[512]{0:T(512)S(1)}, f32[512]{0:T(512)}, u32[]{:S(2)}) copy-start(f32[512]{0:T(512)} %get-tuple-element.106) | copy-start | bytes 6148
  533.0 6.7 %copy-start.8 = (f32[512]{0:T(512)S(1)}, f32[512]{0:T(512)}, u32[]{:S(2)}) copy-start(f32[512]{0:T(512)} %get-tuple-element.107) | copy-start | bytes 6148
  (37 other events, 213.9 us)
Sparse Core Ops, SparseCore 0:
  244.8 123.3 all-gather.4
  377.6 118.0 all-gather.2
